TPU v7x, 32 devices: a whole 2x2x4 slice. The times are simulated.
32 devices in a mesh: row: 4 (over z), col: 8 (over y, x, core).
Axes of the slice: x: 2, y: 2, z: 4, core: 2. Of those that a mesh axis runs over, the one named last changes fastest.
Arguments:
- frontal: float32 [4096, 16384], P('row', 'col'), may hold values from -6 to 6
- sketch: float32 [16384, 256], P('col'), may hold values from -0.046875 to 0.046875
- rank_table: int32 [3, 4], replicated, may hold values from 64 to 256, as said below
Outputs:
- leaf_basis: float32 [4096, 256], P(('row', 'col'))
- top_basis: float32 [4096, 256], P(('row', 'col'))
- coupling: float32 [1024, 16384], P('row', 'col')
Inputs may be any that keep to these rules, and one draw needn't show every extreme that they name: rank_table[l, g] is the rank of the level-l node made of the 2**l consecutive row groups holding g, equal over the groups of that node; a node's rank is at most the larger of its two children's ranks; in every draw some leaf has rank 256 and some leaf rank 256 // 4.
All inputs are finite; a program needn't handle non-finite values.
Results may differ from a plain program's by a relative error of at most 0.00012.
Values sent between devices are 32-bit elements; how exact they have to be, the bound alone decides.
No kernel may reach another device: no remote copies, remote signals or barrier semaphores. Data moves between devices by JAX's collectives and lax.ppermute only.
A program may use at most 64 MiB of HBM per device.

v0:
```python
import jax
import jax.numpy as jnp
from jax import lax
from jax.sharding import PartitionSpec as P

LEVELS = 2


def swapped(block, axis, bit):
    count = lax.axis_size(axis)
    route = []
    for low in range(count):
        high = low | 1 << bit
        if high != low and high < count:
            route += [(low, high), (high, low)]
    return lax.ppermute(block, axis, route)


def product(left, right):
    return jnp.dot(left, right, precision=lax.Precision.HIGHEST, preferred_element_type=jnp.float32)


def mask_of(rank_value, width):
    return (jnp.arange(width) < rank_value).astype(jnp.float32)


def factor(gram_full, keep_mask):
    masked = keep_mask[:, None] * gram_full * keep_mask[None, :] + jnp.diag(1.0 - keep_mask)
    return jnp.linalg.cholesky(masked)


def right_solve(factor_low, operand):
    return lax.linalg.triangular_solve(
        factor_low, operand, left_side=False, lower=True, transpose_a=True
    )


def left_solve(factor_low, operand):
    return lax.linalg.triangular_solve(factor_low, operand, left_side=True, lower=True)


def body(frontal, sketch, rank_table):
    width = sketch.shape[1]
    col_count = lax.axis_size("col")
    share_rows = frontal.shape[0] // col_count
    row_group = lax.axis_index("row")
    column = lax.axis_index("col")
    keep_mask = mask_of(rank_table[0, row_group], width)
    samples = lax.psum(product(frontal, sketch), "col")
    gram_full = product(samples.T, samples)
    factor_low = factor(gram_full, keep_mask)
    full_basis = right_solve(factor_low, samples * keep_mask[None, :])
    coupling = product(full_basis.T, frontal)
    leaf_share = lax.dynamic_slice_in_dim(full_basis, column * share_rows, share_rows, 0)
    coords = left_solve(factor_low, keep_mask[:, None] * gram_full)
    chain_coef = jnp.eye(width, dtype=jnp.float32)
    for height in range(1, LEVELS + 1):
        own_gram = product(coords.T, coords)
        sibling = swapped(own_gram, "row", height - 1)
        pair_gram = own_gram + sibling
        node_mask = mask_of(rank_table[height, row_group], width)
        node_factor = factor(pair_gram, node_mask)
        chain_coef = product(chain_coef, right_solve(node_factor, coords * node_mask[None, :]))
        coords = left_solve(node_factor, node_mask[:, None] * pair_gram)
    top_share = product(leaf_share, chain_coef)
    return (leaf_share, top_share, coupling)


def solution(mesh):
    return jax.shard_map(
        body,
        mesh=mesh,
        in_specs=(P("row", "col"), P("col", None), P()),
        out_specs=(P(("row", "col"), None), P(("row", "col"), None), P("row", "col")),
        check_vma=False,
    )
```

profile of v0, /device:TPU:0, one launch (start us, length us, event | category | flops | bytes accessed | tf_op | source)
XLA Modules:
  0.0 332.8 jit_solution(14702008492156410330)
XLA Ops:
  7.2 1.5 copy-done
  8.8 10.0 %fusion.57 = f32[1024,256]{1,0:T(8,128)} fusion(f32[1024,2048]{1,0:T(8,128)} %param.8, f32[2048,256]{1,0:T(8,128)S(1)} %copy-done), kind=kOutput, calls=%fused_computation.129 | convolution fusion | flops 6442450944 | bytes 11534336 | tf_op jit(solution)/shard_map/dot_general | solution.py:20
  24.5 53.9 %all-reduce.3.cloned.1.call-done = f32[1024,256]{1,0:T(8,128)} async-done(((f32[1024,256]{1,0:T(8,128)}), f32[1024,256]{1,0:T(8,128)}) %all-reduce.3.cloned.1.call-update) | async-done | bytes 1048592 | tf_op jit(solution)/shard_map/psum | solution.py:49
  78.4 4.1 %select_add_fusion.2 = (f32[256,256]{0,1:T(8,128)S(1)}, f32[256,256]{0,1:T(8,128)}) fusion(f32[256]{0:T(256)S(1)} %broadcast_subtract_fusion.2, f32[256]{0:T(256)S(1)} %compare_convert_fusion.2, f32[1024,256]{1,0:T(8,128)} %all-reduce.3.cloned.1.call-done), kind=kOutput, calls=%fused_computation.44 | convolution fusion | flops 805634048 | bytes 1574912 | tf_op jit(solution)/shard_map/dot_general | solution.py:20
  85.1 11.7 %cholesky.172 = f32[128,128]{1,0:T(8,128)S(1)} custom-call(f32[128,128]{1,0:T(8,128)S(1)} %cholesky.270), custom_call_target="Cholesky" | custom-call | tf_op jit(solution)/shard_map/jit(cholesky)/cholesky | solution.py:29
  97.0 9.8 %custom-call.22 = f32[1,128,128]{1,2,0:T(8,128)S(1)} custom-call(f32[1,128,128]{2,1,0:T(8,128)S(1)} %get-tuple-element.98), custom_call_target="InvertDiagBlocksLowerTriangular" | custom-call | tf_op jit(solution)/shard_map/jit(cholesky)/cholesky | solution.py:29
  109.0 11.9 %cholesky.189 = f32[128,128]{1,0:T(8,128)S(1)} custom-call(f32[128,128]{1,0:T(8,128)S(1)} %convolution_subtract_fusion.6), custom_call_target="Cholesky" | custom-call | tf_op jit(solution)/shard_map/jit(cholesky)/cholesky | solution.py:29
  125.2 6.8 %while.9 = (s32[]{:T(128)}, f32[256,256]{0,1:T(8,128)S(1)}, s32[2,2]{1,0:T(2,128)}, f32[2,128,128]{2,1,0:T(8,128)}, s32[]{:T(128)}) while((s32[]{:T(128)}, f32[256,256]{0,1:T(8,128)S(1)}, s32[2,2]{1,0:T(2,128)}, f32[2,128,128]{2,1,0:T(8,128)}, s32[]{:T(128)}) %tuple.79), condition=%wide.while_cond.2, body=%wide.while_body.2.sunk | while | flops 2 | bytes 393329 | solution.py:33
  126.5 1.3 dynamic-slice.25
  132.0 21.1 %custom-call.17 = f32[2,128,128]{1,2,0:T(8,128)} custom-call(f32[2,128,128]{2,1,0:T(8,128)} %get-tuple-element.29), custom_call_target="InvertDiagBlocksLowerTriangular" | custom-call | tf_op jit(solution)/shard_map/triangular_solve | solution.py:33
  154.4 2.0 convolution_subtract_fusion.3
  158.3 2.2 fusion.18
  160.4 1.4 collective-permute-start
  162.0 1.5 fusion.1
  164.4 1.5 fusion.42
  166.7 10.9 %fusion = f32[256,2048]{1,0:T(8,128)} fusion(f32[1024,2048]{1,0:T(8,128)} %param.8, f32[1024,128]{0,1:T(8,128)S(1)} %fusion.42, f32[1024,128]{0,1:T(8,128)S(1)} %fusion.1), kind=kOutput, calls=%fused_computation.17 | convolution fusion | flops 6442713088 | bytes 11534336 | tf_op jit(solution)/shard_map/dot_general | solution.py:20
  179.7 11.7 %cholesky.206 = f32[128,128]{1,0:T(8,128)S(1)} custom-call(f32[128,128]{1,0:T(8,128)S(1)} %cholesky.273), custom_call_target="Cholesky" | custom-call | tf_op jit(solution)/shard_map/jit(cholesky)/cholesky | solution.py:29
  192.1 9.8 %custom-call.24 = f32[1,128,128]{1,2,0:T(8,128)S(1)} custom-call(f32[1,128,128]{2,1,0:T(8,128)S(1)} %get-tuple-element.96), custom_call_target="InvertDiagBlocksLowerTriangular" | custom-call | tf_op jit(solution)/shard_map/jit(cholesky)/cholesky | solution.py:29
  204.1 11.7 %cholesky.223 = f32[128,128]{1,0:T(8,128)S(1)} custom-call(f32[128,128]{1,0:T(8,128)S(1)} %convolution_subtract_fusion.5), custom_call_target="Cholesky" | custom-call | tf_op jit(solution)/shard_map/jit(cholesky)/cholesky | solution.py:29
  217.9 5.4 %while.10 = (s32[]{:T(128)}, f32[256,256]{1,0:T(8,128)S(1)}, s32[2,2]{1,0:T(2,128)}, f32[2,128,128]{2,1,0:T(8,128)S(1)}, s32[]{:T(128)}) while((s32[]{:T(128)}, f32[256,256]{1,0:T(8,128)S(1)}, s32[2,2]{1,0:T(2,128)}, f32[2,128,128]{2,1,0:T(8,128)S(1)}, s32[]{:T(128)}) %tuple.82), condition=%wide.while_cond.1, body=%wide.while_body.1.sunk | while | flops 2 | bytes 131189 | solution.py:33
  219.2 1.4 bitcast_dynamic-update-slice_fusion.7
  221.9 1.4 bitcast_dynamic-update-slice_fusion.7
  223.3 19.8 %custom-call.25 = f32[2,128,128]{1,2,0:T(8,128)S(1)} custom-call(f32[2,128,128]{2,1,0:T(8,128)S(1)} %get-tuple-element.43), custom_call_target="InvertDiagBlocksLowerTriangular" | custom-call | tf_op jit(solution)/shard_map/triangular_solve/custom-call.5 | solution.py:33
  245.3 2.5 collective-permute-start.1
  248.4 10.4 %collective-permute-done.1 = f32[256,256]{0,1:T(8,128)S(1)} collective-permute-done((f32[256,256]{0,1:T(8,128)S(1)}, f32[256,256]{0,1:T(8,128)S(1)}, u32[]{:S(2)}, u32[]{:S(2)}) %collective-permute-start.1) | collective-permute-done | bytes 262176 | tf_op jit(solution)/shard_map/ppermute | solution.py:16
  259.8 11.7 %cholesky.240 = f32[128,128]{1,0:T(8,128)S(1)} custom-call(f32[128,128]{1,0:T(8,128)S(1)} %cholesky.276), custom_call_target="Cholesky" | custom-call | tf_op jit(solution)/shard_map/jit(cholesky)/cholesky | solution.py:29
  272.2 9.8 %custom-call.27 = f32[1,128,128]{1,2,0:T(8,128)S(1)} custom-call(f32[1,128,128]{2,1,0:T(8,128)S(1)} %get-tuple-element.92), custom_call_target="InvertDiagBlocksLowerTriangular" | custom-call | tf_op jit(solution)/shard_map/jit(cholesky)/cholesky | solution.py:29
  284.2 11.9 %cholesky.257 = f32[128,128]{1,0:T(8,128)S(1)} custom-call(f32[128,128]{1,0:T(8,128)S(1)} %convolution_subtract_fusion.4), custom_call_target="Cholesky" | custom-call | tf_op jit(solution)/shard_map/jit(cholesky)/cholesky | solution.py:29
  298.3 5.4 %while.11 = (s32[]{:T(128)}, f32[256,256]{1,0:T(8,128)S(1)}, s32[2,2]{1,0:T(2,128)}, f32[2,128,128]{2,1,0:T(8,128)S(1)}, s32[]{:T(128)}) while((s32[]{:T(128)}, f32[256,256]{1,0:T(8,128)S(1)}, s32[2,2]{1,0:T(2,128)}, f32[2,128,128]{2,1,0:T(8,128)S(1)}, s32[]{:T(128)}) %tuple.85), condition=%wide.while_cond.1.clone, body=%wide.while_body.1.clone.sunk | while | flops 2 | bytes 131189 | solution.py:33
  299.5 1.4 bitcast_dynamic-update-slice_fusion.8
  302.2 1.4 bitcast_dynamic-update-slice_fusion.8
  303.7 19.7 %custom-call.28 = f32[2,128,128]{1,2,0:T(8,128)S(1)} custom-call(f32[2,128,128]{2,1,0:T(8,128)S(1)} %get-tuple-element.45), custom_call_target="InvertDiagBlocksLowerTriangular" | custom-call | tf_op jit(solution)/shard_map/triangular_solve/custom-call.5 | solution.py:33
  (109 shorter events, 44.3 us)
Async XLA Ops:
  7.2 1.6 copy-start
  7.2 11.6 %copy-start.7 = (s32[3,4]{1,0:T(4,128)S(1)}, s32[3,4]{1,0:T(4,128)}, u32[]{:S(2)}) copy-start(s32[3,4]{1,0:T(4,128)} %param.10) | copy-start | bytes 148
  7.2 71.2 %all-reduce.3.cloned.1.call-start = ((), (), s32[]{:S(2)}) async-start(), calls=%async_computation | async-start | bytes 2097152 | tf_op jit(solution)/shard_map/psum | solution.py:49
  78.4 83.5 %copy-start.1 = (f32[1024,256]{1,0:T(8,128)S(1)}, f32[1024,256]{1,0:T(8,128)}, u32[]{:S(2)}) copy-start(f32[1024,256]{1,0:T(8,128)} %all-reduce.3.cloned.1.call-done) | copy-start | bytes 3145732
  84.4 0.7 copy-start.4
  158.3 6.1 %copy-start.2 = (f32[128,256]{0,1:T(8,128)}, f32[128,256]{0,1:T(8,128)S(1)}, u32[]{:S(2)}) copy-start(f32[128,256]{0,1:T(8,128)S(1)} %fusion.41) | copy-start | bytes 393220
  160.4 17.2 %collective-permute-start = (f32[256,256]{0,1:T(8,128)}, f32[256,256]{0,1:T(8,128)}, u32[]{:S(2)}, u32[]{:S(2)}) collective-permute-start(f32[256,256]{0,1:T(8,128)} %fusion.18), channel_id=1, source_target_pairs={{0,8},{8,0},{16,24},{24,16},{1,9},{9,1},{17,25},{25,17},{2,10},{10... | collective-permute-start | bytes 786440 | tf_op jit(solution)/shard_map/ppermute | solution.py:16
  161.9 15.7 %copy-start.8 = (f32[256]{0:T(256)S(1)}, f32[256]{0:T(256)}, u32[]{:S(2)}) copy-start(f32[256]{0:T(256)} %broadcast_subtract_fusion.1) | copy-start | bytes 3076
  165.9 11.8 %copy-start.3 = (f32[128,256]{0,1:T(8,128)S(1)}, f32[128,256]{0,1:T(8,128)}, u32[]{:S(2)}) copy-start(f32[128,256]{0,1:T(8,128)} %copy-done.2) | copy-start | bytes 393220
  179.0 0.7 copy-start.5
  245.3 13.5 %collective-permute-start.1 = (f32[256,256]{0,1:T(8,128)S(1)}, f32[256,256]{0,1:T(8,128)S(1)}, u32[]{:S(2)}, u32[]{:S(2)}) collective-permute-start(f32[256,256]{0,1:T(8,128)S(1)} %fusion.16), channel_id=1, source_target_pairs={{0,16},{16,0},{8,24},{24,8},{1,17},{17,1},{9,25},{25,9},{2,18},{18... | collective-permute-start | bytes 786440 | tf_op jit(solution)/shard_map/ppermute | solution.py:16
  259.1 0.7 copy-start.6
Sparse Core Ops, SparseCore 0:
  18.9 59.4 all-reduce.2
where the time goes:
time: 337 us; the launch traced here: 333 us
  other arithmetic  172 us (51%)
  waiting for transfers between devices  64.3 us (19%)
  matrix products  47 us (14%)
  local copies, waits for them, and re-layouts  26.8 us (8%)
  between operations  18.8 us (6%)
  starting transfers between devices  3.94 us (1%)
    another operation x20, other arithmetic, factor(): return jnp.linalg.cholesky(masked)  104 us
    another operation x8, other arithmetic, right_solve(): lax.linalg.triangular_solve(factor_low, operand, left_side=False, lower=T...  61.3 us
    psum x1, waiting for transfers between devices, body(): samples = lax.psum(product(frontal, sketch), 'col')  53.9 us
    dot_general x8, matrix products, product(): jnp.dot(left, right, precision=lax.Precision.HIGHEST, preferred_element_t...  29.4 us
    another operation x13, local copies, waits for them, and re-layouts, right_solve(): lax.linalg.triangular_solve(factor_low, operand, left_side=False, lower=T...  12 us
    ppermute x2, waiting for transfers between devices, swapped(): return lax.ppermute(block, axis, route)  10.4 us
    another operation x10, local copies, waits for them, and re-layouts  6.8 us
  transfers between devices with their start and end apart: 3, of which 2 were waited for; matrix products, arithmetic and copies ran while one was open for 7% of the time, Pallas kernels for 0%

commit v1 on v0

--- a/solution.py
+++ b/solution.py
@@ -46,7 +46,7 @@
     row_group = lax.axis_index("row")
     column = lax.axis_index("col")
     keep_mask = mask_of(rank_table[0, row_group], width)
-    samples = lax.psum(product(frontal, sketch), "col")
+    samples = jnp.sum(lax.all_gather(product(frontal, sketch), "col"), axis=0)
     gram_full = product(samples.T, samples)
     factor_low = factor(gram_full, keep_mask)
     full_basis = right_solve(factor_low, samples * keep_mask[None, :])

time: 337 us -> 325 us (0.964)
  local copies, waits for them, and re-layouts: 26.8 us -> 19.4 us
  matrix products: 47 us -> 42.2 us
    psum x1 -> x0, waiting for transfers between devices: 53.9 us -> none  [body(): samples = lax.psum(product(frontal, sketch), 'col')]
    all_gather x0 -> x1, waiting for transfers between devices: none -> 52.3 us  [body(): samples = jnp.sum(lax.all_gather(product(frontal, sketch), 'col'), axis=0)]
    reduce_sum x0 -> x1, other arithmetic: none -> 4.06 us  [body(): samples = jnp.sum(lax.all_gather(product(frontal, sketch), 'col'), axis=0)]
    dot_general x8, matrix products: 29.4 us -> 26.1 us  [product(): jnp.dot(left, right, precision=lax.Precision.HIGHEST, preferred_element_t...]
  transfers between devices with their start and end apart: 3 -> 3, of which waited for: 2 -> 2; matrix products, arithmetic and copies ran while one was open for 7% -> 5% of each run, Pallas kernels for 0% -> 0%
where the time goes in v1:
time: 325 us; the launch traced here: 321 us
  other arithmetic  173 us (53%)
  waiting for transfers between devices  64 us (20%)
  matrix products  42.2 us (13%)
  local copies, waits for them, and re-layouts  19.4 us (6%)
  between operations  18.8 us (6%)
  starting transfers between devices  4.06 us (1%)
    another operation x20, other arithmetic, factor(): return jnp.linalg.cholesky(masked)  104 us
    another operation x8, other arithmetic, right_solve(): lax.linalg.triangular_solve(factor_low, operand, left_side=False, lower=T...  59.8 us
    all_gather x1, waiting for transfers between devices, body(): samples = jnp.sum(lax.all_gather(product(frontal, sketch), 'col'), axis=0)  52.3 us
    dot_general x8, matrix products, product(): jnp.dot(left, right, precision=lax.Precision.HIGHEST, preferred_element_t...  26.1 us
    ppermute x2, waiting for transfers between devices, swapped(): return lax.ppermute(block, axis, route)  11.6 us
    another operation x13, local copies, waits for them, and re-layouts, right_solve(): lax.linalg.triangular_solve(factor_low, operand, left_side=False, lower=T...  10.1 us
  transfers between devices with their start and end apart: 3, of which 2 were waited for; matrix products, arithmetic and copies ran while one was open for 5% of the time, Pallas kernels for 0%

profile of v1, /device:TPU:0, one launch (start us, length us, event | category | flops | bytes accessed | tf_op | source)
XLA Modules:
  0.0 321.3 jit_solution(6011935369781617394)
XLA Ops:
  7.2 1.5 copy-done
  8.8 10.0 %fusion.57 = f32[1024,256]{1,0:T(8,128)} fusion(f32[1024,2048]{1,0:T(8,128)} %param.8, f32[2048,256]{1,0:T(8,128)S(1)} %copy-done), kind=kOutput, calls=%fused_computation.129 | convolution fusion | flops 6442450944 | bytes 11534336 | tf_op jit(solution)/shard_map/dot_general | solution.py:20
  23.6 52.3 %all-gather.3.cloned.1.call-done = f32[8192,256]{1,0:T(8,128)} async-done(((f32[1024,256]{1,0:T(8,128)}), f32[8192,256]{1,0:T(8,128)}) %all-gather.3.cloned.1.call-update) | async-done | bytes 8388624 | tf_op jit(solution)/shard_map/all_gather | solution.py:49
  75.9 4.1 %reduce_sum.9 = f32[1024,256]{1,0:T(8,128)S(1)} reduce(f32[8,1024,256]{2,1,0:T(8,128)} %bitcast.122, f32[]{:T(128)} %constant.84.clone.1), dimensions={0}, to_apply=%region_0.0 | reduce | flops 1835008 | bytes 9437188 | tf_op jit(solution)/shard_map/reduce_sum | solution.py:49
  81.0 2.5 select_add_fusion.2
  83.7 11.7 %cholesky.172 = f32[128,128]{1,0:T(8,128)S(1)} custom-call(f32[128,128]{1,0:T(8,128)S(1)} %cholesky.270), custom_call_target="Cholesky" | custom-call | tf_op jit(solution)/shard_map/jit(cholesky)/cholesky | solution.py:29
  95.6 9.8 %custom-call.22 = f32[1,128,128]{1,2,0:T(8,128)S(1)} custom-call(f32[1,128,128]{2,1,0:T(8,128)S(1)} %get-tuple-element.98), custom_call_target="InvertDiagBlocksLowerTriangular" | custom-call | tf_op jit(solution)/shard_map/jit(cholesky)/cholesky | solution.py:29
  106.0 11.9 %cholesky.189 = f32[128,128]{1,0:T(8,128)S(1)} custom-call(f32[128,128]{1,0:T(8,128)S(1)} %convolution_subtract_fusion.6), custom_call_target="Cholesky" | custom-call | tf_op jit(solution)/shard_map/jit(cholesky)/cholesky | solution.py:29
  120.8 4.2 %while.9 = (s32[]{:T(128)}, f32[256,256]{0,1:T(8,128)S(1)}, s32[2,2]{1,0:T(2,128)S(1)}, f32[2,128,128]{2,1,0:T(8,128)S(1)}, s32[]{:T(128)}) while((s32[]{:T(128)}, f32[256,256]{0,1:T(8,128)S(1)}, s32[2,2]{1,0:T(2,128)S(1)}, f32[2,128,128]{2,1,0:T(8,128)S(1)}, s32[]{:T(128)}) %tuple.79), condition=%wide.while_cond.2, body=%wide.while_body.2.sunk | while | flops 2 | bytes 393329 | solution.py:33
  121.4 1.4 dynamic-slice.25
  125.0 19.7 %custom-call.17 = f32[2,128,128]{1,2,0:T(8,128)S(1)} custom-call(f32[2,128,128]{2,1,0:T(8,128)S(1)} %get-tuple-element.29), custom_call_target="InvertDiagBlocksLowerTriangular" | custom-call | tf_op jit(solution)/shard_map/triangular_solve | solution.py:33
  145.9 2.0 convolution_subtract_fusion.3
  148.0 1.7 fusion.1
  149.6 2.0 convolution_subtract_fusion
  154.7 1.6 collective-permute-start
  156.3 10.9 %fusion = f32[256,2048]{1,0:T(8,128)} fusion(f32[1024,2048]{1,0:T(8,128)} %param.8, f32[1024,128]{0,1:T(8,128)S(1)} %fusion.42, f32[1024,128]{0,1:T(8,128)S(1)} %fusion.1), kind=kOutput, calls=%fused_computation.17 | convolution fusion | flops 6442713088 | bytes 11534336 | tf_op jit(solution)/shard_map/dot_general | solution.py:20
  168.2 11.7 %cholesky.206 = f32[128,128]{1,0:T(8,128)S(1)} custom-call(f32[128,128]{1,0:T(8,128)S(1)} %cholesky.273), custom_call_target="Cholesky" | custom-call | tf_op jit(solution)/shard_map/jit(cholesky)/cholesky | solution.py:29
  180.0 9.8 %custom-call.24 = f32[1,128,128]{1,2,0:T(8,128)S(1)} custom-call(f32[1,128,128]{2,1,0:T(8,128)S(1)} %get-tuple-element.96), custom_call_target="InvertDiagBlocksLowerTriangular" | custom-call | tf_op jit(solution)/shard_map/jit(cholesky)/cholesky | solution.py:29
  191.9 11.7 %cholesky.223 = f32[128,128]{1,0:T(8,128)S(1)} custom-call(f32[128,128]{1,0:T(8,128)S(1)} %convolution_subtract_fusion.5), custom_call_target="Cholesky" | custom-call | tf_op jit(solution)/shard_map/jit(cholesky)/cholesky | solution.py:29
  206.4 4.1 %while.10 = (s32[]{:T(128)}, f32[256,256]{1,0:T(8,128)S(1)}, s32[2,2]{1,0:T(2,128)S(1)}, f32[2,128,128]{2,1,0:T(8,128)S(1)}, s32[]{:T(128)}) while((s32[]{:T(128)}, f32[256,256]{1,0:T(8,128)S(1)}, s32[2,2]{1,0:T(2,128)S(1)}, f32[2,128,128]{2,1,0:T(8,128)S(1)}, s32[]{:T(128)}) %tuple.90), condition=%wide.while_cond.1, body=%wide.while_body.1.sunk | while | flops 2 | bytes 131189 | solution.py:33
  207.1 1.4 bitcast_dynamic-update-slice_fusion.7
  209.1 1.4 bitcast_dynamic-update-slice_fusion.7
  210.6 19.8 %custom-call.25 = f32[2,128,128]{1,2,0:T(8,128)S(1)} custom-call(f32[2,128,128]{2,1,0:T(8,128)S(1)} %get-tuple-element.43), custom_call_target="InvertDiagBlocksLowerTriangular" | custom-call | tf_op jit(solution)/shard_map/triangular_solve/custom-call.5 | solution.py:33
  232.5 2.5 collective-permute-start.1
  235.6 11.6 %collective-permute-done.1 = f32[256,256]{0,1:T(8,128)S(1)} collective-permute-done((f32[256,256]{0,1:T(8,128)S(1)}, f32[256,256]{0,1:T(8,128)S(1)}, u32[]{:S(2)}, u32[]{:S(2)}) %collective-permute-start.1) | collective-permute-done | bytes 262176 | tf_op jit(solution)/shard_map/ppermute | solution.py:16
  248.2 11.7 %cholesky.240 = f32[128,128]{1,0:T(8,128)S(1)} custom-call(f32[128,128]{1,0:T(8,128)S(1)} %cholesky.276), custom_call_target="Cholesky" | custom-call | tf_op jit(solution)/shard_map/jit(cholesky)/cholesky | solution.py:29
  260.0 9.8 %custom-call.27 = f32[1,128,128]{1,2,0:T(8,128)S(1)} custom-call(f32[1,128,128]{2,1,0:T(8,128)S(1)} %get-tuple-element.92), custom_call_target="InvertDiagBlocksLowerTriangular" | custom-call | tf_op jit(solution)/shard_map/jit(cholesky)/cholesky | solution.py:29
  272.0 11.9 %cholesky.257 = f32[128,128]{1,0:T(8,128)S(1)} custom-call(f32[128,128]{1,0:T(8,128)S(1)} %convolution_subtract_fusion.4), custom_call_target="Cholesky" | custom-call | tf_op jit(solution)/shard_map/jit(cholesky)/cholesky | solution.py:29
  286.7 5.4 %while.11 = (s32[]{:T(128)}, f32[256,256]{1,0:T(8,128)S(1)}, s32[2,2]{1,0:T(2,128)}, f32[2,128,128]{2,1,0:T(8,128)S(1)}, s32[]{:T(128)}) while((s32[]{:T(128)}, f32[256,256]{1,0:T(8,128)S(1)}, s32[2,2]{1,0:T(2,128)}, f32[2,128,128]{2,1,0:T(8,128)S(1)}, s32[]{:T(128)}) %tuple.91), condition=%wide.while_cond.1.clone, body=%wide.while_body.1.clone.sunk | while | flops 2 | bytes 131189 | solution.py:33
  288.0 1.4 bitcast_dynamic-update-slice_fusion.8
  290.7 1.4 bitcast_dynamic-update-slice_fusion.8
  292.1 19.7 %custom-call.28 = f32[2,128,128]{1,2,0:T(8,128)S(1)} custom-call(f32[2,128,128]{2,1,0:T(8,128)S(1)} %get-tuple-element.45), custom_call_target="InvertDiagBlocksLowerTriangular" | custom-call | tf_op jit(solution)/shard_map/triangular_solve/custom-call.5 | solution.py:33
  (104 shorter events, 33.3 us)
Async XLA Ops:
  7.2 1.6 copy-start
  7.2 11.6 %copy-start.3 = (s32[3,4]{1,0:T(4,128)S(1)}, s32[3,4]{1,0:T(4,128)}, u32[]{:S(2)}) copy-start(s32[3,4]{1,0:T(4,128)} %param.10) | copy-start | bytes 148
  7.2 68.8 %all-gather.3.cloned.1.call-start = ((), (), s32[]{:S(2)}) async-start(), calls=%async_computation | async-start | bytes 9437184 | tf_op jit(solution)/shard_map/all_gather | solution.py:49
  125.0 24.6 %copy-start.4 = (s32[2,2]{1,0:T(2,128)}, s32[2,2]{1,0:T(2,128)S(1)}, u32[]{:S(2)}) copy-start(s32[2,2]{1,0:T(2,128)S(1)} %get-tuple-element.256) | copy-start | bytes 52
  154.3 52.2 %copy-start.5 = (s32[2,2]{1,0:T(2,128)S(1)}, s32[2,2]{1,0:T(2,128)}, u32[]{:S(2)}) copy-start(s32[2,2]{1,0:T(2,128)} %copy-done.4) | copy-start | bytes 52
  154.7 12.5 %collective-permute-start = (f32[256,256]{0,1:T(8,128)S(1)}, f32[256,256]{0,1:T(8,128)S(1)}, u32[]{:S(2)}, u32[]{:S(2)}) collective-permute-start(f32[256,256]{0,1:T(8,128)S(1)} %fusion.18), channel_id=1, source_target_pairs={{0,8},{8,0},{16,24},{24,16},{1,9},{9,1},{17,25},{25,17},{2,10},{10... | collective-permute-start | bytes 786440 | tf_op jit(solution)/shard_map/ppermute | solution.py:16
  167.5 0.7 copy-start.1
  232.5 14.7 %collective-permute-start.1 = (f32[256,256]{0,1:T(8,128)S(1)}, f32[256,256]{0,1:T(8,128)S(1)}, u32[]{:S(2)}, u32[]{:S(2)}) collective-permute-start(f32[256,256]{0,1:T(8,128)S(1)} %fusion.16), channel_id=1, source_target_pairs={{0,16},{16,0},{8,24},{24,8},{1,17},{17,1},{9,25},{25,9},{2,18},{18... | collective-permute-start | bytes 786440 | tf_op jit(solution)/shard_map/ppermute | solution.py:16
  247.5 0.7 copy-start.2
Sparse Core Ops, SparseCore 0:
  18.9 56.9 all-gather.2
